TPU v7x, 128 devices: a whole 4x4x4 slice. The times are simulated.
128 devices in a mesh: row: 16 (over y, x), col: 8 (over z, core).
Axes of the slice: x: 4, y: 4, z: 4, core: 2. Of those that a mesh axis runs over, the one named last changes fastest.
Arguments:
- layer_input: bfloat16 [768, 8192], P('col', 'row'), may hold values from -6 to 6
- out_grad: bfloat16 [768, 8192], P('col', 'row'), may hold values from -6 to 6
- gate_weight: bfloat16 [8192, 28672], P('row', 'col'), may hold values from -0.0625 to 0.0625
- up_weight: bfloat16 [8192, 28672], P('row', 'col'), may hold values from -0.0625 to 0.0625
- down_weight: bfloat16 [28672, 8192], P('col', 'row'), may hold values from -0.03125 to 0.03125
Outputs:
- input_grad: bfloat16 [768, 8192], P('col', 'row')
- gate_grad: bfloat16 [8192, 28672], P('row', 'col')
- up_grad: bfloat16 [8192, 28672], P('row', 'col')
- down_grad: bfloat16 [28672, 8192], P('col', 'row')
All inputs are finite; a program needn't handle non-finite values.
Results may differ from a plain program's by a relative error of at most 0.033.
Values may be sent and summed in bfloat16 or wider, within the bound.
A program may use at most 192 MiB of HBM per device.

v0:
```python
import jax
import jax.numpy as jnp
from jax import lax
from jax.sharding import PartitionSpec as P


def swiglu_back(summed, width):
    gate = summed[:, :width]
    up = summed[:, width : 2 * width]
    hidden_grad = summed[:, 2 * width :]
    sigma = jax.nn.sigmoid(gate)
    swish = gate * sigma
    hidden = (swish * up).astype(jnp.bfloat16)
    up_delta = (hidden_grad * swish).astype(jnp.bfloat16)
    gate_delta = (hidden_grad * up * sigma * (1.0 + gate * (1.0 - sigma))).astype(jnp.bfloat16)
    return (hidden, gate_delta, up_delta)


def local(layer_input, out_grad, gate_weight, up_weight, down_weight):
    input_rows, cot_rows = (
        lax.all_gather(layer_input, "col", axis=0, tiled=True),
        lax.all_gather(out_grad, "col", axis=0, tiled=True),
    )
    tokens = input_rows.shape[0]
    width = gate_weight.shape[1]
    both_weights = jnp.concatenate([gate_weight, up_weight], axis=1)
    contract_last = (((1,), (1,)), ((), ()))
    contract_first = (((0,), (0,)), ((), ()))
    left = input_rows
    right = cot_rows
    gate_up = jnp.dot(left, both_weights, preferred_element_type=jnp.float32)
    hidden_grad = lax.dot_general(
        right, down_weight, contract_last, preferred_element_type=jnp.float32
    )
    summed = lax.psum_scatter(
        jnp.concatenate([gate_up, hidden_grad], axis=1).astype(jnp.bfloat16),
        "row",
        scatter_dimension=0,
        tiled=True,
    ).astype(jnp.float32)
    hidden, gate_delta, up_delta = swiglu_back(summed, width)
    accumulate_hidden = lax.all_gather(hidden, "row", axis=0, tiled=True)
    accumulate_gate_delta = lax.all_gather(gate_delta, "row", axis=0, tiled=True)
    accumulate_up_delta = lax.all_gather(up_delta, "row", axis=0, tiled=True)
    left = input_rows
    right = cot_rows
    down_sum = lax.dot_general(
        accumulate_hidden, right, contract_first, preferred_element_type=jnp.float32
    )
    gate_sum = lax.dot_general(
        left, accumulate_gate_delta, contract_first, preferred_element_type=jnp.float32
    )
    up_sum = lax.dot_general(
        left, accumulate_up_delta, contract_first, preferred_element_type=jnp.float32
    )
    term = lax.dot_general(
        accumulate_gate_delta, gate_weight, contract_last, preferred_element_type=jnp.float32
    )
    term = term + lax.dot_general(
        accumulate_up_delta, up_weight, contract_last, preferred_element_type=jnp.float32
    )
    factor = 1.0 / tokens**0.5
    down_grad = (down_sum * factor).astype(jnp.bfloat16)
    gate_grad = (gate_sum * factor).astype(jnp.bfloat16)
    up_grad = (up_sum * factor).astype(jnp.bfloat16)
    input_grad = lax.psum_scatter(term.astype(jnp.bfloat16), "col", scatter_dimension=0, tiled=True)
    return (input_grad, gate_grad, up_grad, down_grad)


def solution(mesh):
    placed = (P("col", "row"), P("col", "row"), P("row", "col"), P("row", "col"), P("col", "row"))
    return jax.shard_map(
        local,
        mesh=mesh,
        in_specs=placed,
        out_specs=(P("col", "row"), P("row", "col"), P("row", "col"), P("col", "row")),
        check_vma=False,
    )
```

profile of v0, /device:TPU:0, one launch (start us, length us, event | category | flops | bytes accessed | tf_op | source)
XLA Modules:
  0.0 429.2 jit_solution(3540597175312089114)
XLA Ops:
  7.2 0.0 reduce-scatter.7.cloned.1.call-start
  7.2 14.9 %all_gather.15 = bf16[768,512]{1,0:T(8,128)(2,1)S(1)} all-gather(bf16[96,512]{1,0:T(8,128)(2,1)} %param.5), channel_id=1, replica_groups=mesh['row'=16,'col'=8] {'col'}, dimensions={0}, use_global_device_ids=true | all-gather | bytes 884736 | tf_op jit(solution)/shard_map/all_gather | solution.py:21
  22.1 13.6 %all_gather.16 = bf16[768,512]{1,0:T(8,128)(2,1)S(1)} all-gather(bf16[96,512]{1,0:T(8,128)(2,1)} %param.6), channel_id=1, replica_groups=mesh['row'=16,'col'=8] {'col'}, dimensions={0}, use_global_device_ids=true | all-gather | bytes 884736 | tf_op jit(solution)/shard_map/all_gather | solution.py:22
  35.7 7.5 %convolution_convert_fusion.1 = bf16[768,3584]{0,1:T(8,128)(2,1)} fusion(bf16[768,512]{1,0:T(8,128)(2,1)S(1)} %all_gather.16, bf16[3584,512]{1,0:T(8,128)(2,1)} %param.9), kind=kOutput, calls=%fused_computation.9 | convolution fusion | flops 2821324800 | bytes 9961472 | tf_op jit(solution)/shard_map/dot_general | solution.py:32
  43.2 13.8 %fusion = bf16[768,7168]{0,1:T(8,128)(2,1)} fusion(bf16[768,512]{1,0:T(8,128)(2,1)S(1)} %all_gather.15, bf16[512,3584]{1,0:T(8,128)(2,1)} %param.8, bf16[512,3584]{1,0:T(8,128)(2,1)} %param.7), kind=kOutput, calls=%fused_computation.2 | convolution fusion | flops 5657329664 | bytes 19136512 | tf_op jit(solution)/shard_map/dot_general | solution.py:31
  57.0 18.5 %pad_maximum_fusion = bf16[768,10752]{0,1:T(8,128)(2,1)} fusion(bf16[768,3584]{0,1:T(8,128)(2,1)} %convolution_convert_fusion.1, bf16[768,7168]{0,1:T(8,128)(2,1)} %fusion), kind=kLoop, calls=%fused_computation | loop fusion | flops 33030144 | bytes 33030144 | tf_op jit(solution)/shard_map/concatenate | solution.py:36
  75.5 22.3 %copy.23 = bf16[768,10752]{1,0:T(8,128)(2,1)} copy(bf16[768,10752]{0,1:T(8,128)(2,1)} %pad_maximum_fusion) | data formatting | bytes 33030144
  97.8 0.0 reduce-scatter.7.cloned.1.call-update
  97.8 0.0 all-gather.4.cloned.1.call-start
  97.9 110.7 %reduce-scatter.7.cloned.1.call-done = bf16[48,10752]{1,0:T(8,128)(2,1)} async-done(((bf16[768,10752]{1,0:T(8,128)(2,1)}), bf16[48,10752]{1,0:T(8,128)(2,1)}) %reduce-scatter.7.cloned.1.call-update) | async-done | bytes 1032208 | tf_op jit(solution)/shard_map/reduce_scatter | solution.py:35
  208.6 1.4 convert_element_type.31
  210.0 1.3 multiply_convert_fusion.3
  211.3 0.0 all-gather.4.cloned.1.call-update
  211.3 0.0 all-gather.6.cloned.1.call-start
  211.3 0.7 all-gather.6.cloned.1.call-update
  212.0 0.0 all-gather.8.cloned.1.call-start
  212.1 0.5 all-gather.8.cloned.1.call-update
  212.6 0.2 reduce-scatter.5.cloned.1.call-start
  212.8 55.8 %all-gather.4.cloned.1.call-done = bf16[768,3584]{1,0:T(8,128)(2,1)} async-done(((bf16[48,3584]{1,0:T(8,128)(2,1)}), bf16[768,3584]{1,0:T(8,128)(2,1)}) %all-gather.4.cloned.1.call-update) | async-done | bytes 5505040 | tf_op jit(solution)/shard_map/all_gather | solution.py:43
  268.6 6.1 %fusion.8 = f32[768,512]{1,0:T(8,128)S(1)} fusion(bf16[768,3584]{1,0:T(8,128)(2,1)} %all-gather.4.cloned.1.call-done, bf16[512,3584]{1,0:T(8,128)(2,1)} %param.7), kind=kOutput, calls=%fused_computation.19 | convolution fusion | flops 2818572288 | bytes 10747904 | tf_op jit(solution)/shard_map/dot_general | solution.py:56
  274.8 54.1 %all-gather.6.cloned.1.call-done = bf16[768,3584]{1,0:T(8,128)(2,1)} async-done(((bf16[48,3584]{1,0:T(8,128)(2,1)}), bf16[768,3584]{1,0:T(8,128)(2,1)}) %all-gather.6.cloned.1.call-update) | async-done | bytes 5505040 | tf_op jit(solution)/shard_map/all_gather | solution.py:44
  328.8 7.6 %add_convert_fusion = bf16[768,512]{1,0:T(8,128)(2,1)} fusion(f32[768,512]{1,0:T(8,128)S(1)} %fusion.8, bf16[768,3584]{1,0:T(8,128)(2,1)} %all-gather.6.cloned.1.call-done, bf16[512,3584]{1,0:T(8,128)(2,1)} %param.8), kind=kOutput, calls=%fused_computation.12 | convolution fusion | flops 2819358720 | bytes 11534336 | tf_op jit(solution)/shard_map/dot_general | solution.py:59
  336.4 0.0 reduce-scatter.5.cloned.1.call-update
  336.5 7.1 %fusion.5 = bf16[512,3584]{0,1:T(8,128)(2,1)} fusion(bf16[768,3584]{1,0:T(8,128)(2,1)} %all-gather.6.cloned.1.call-done, bf16[768,512]{1,0:T(8,128)(2,1)S(1)} %all_gather.15), kind=kOutput, calls=%fused_computation.11 | convolution fusion | flops 2822242304 | bytes 9961472 | tf_op jit(solution)/shard_map/dot_general | solution.py:53
  343.6 5.9 %copy.21 = bf16[512,3584]{1,0:T(8,128)(2,1)} copy(bf16[512,3584]{0,1:T(8,128)(2,1)} %fusion.5) | data formatting | bytes 7340032
  349.5 7.1 %fusion.4 = bf16[512,3584]{0,1:T(8,128)(2,1)} fusion(bf16[768,3584]{1,0:T(8,128)(2,1)} %all-gather.4.cloned.1.call-done, bf16[768,512]{1,0:T(8,128)(2,1)S(1)} %all_gather.15), kind=kOutput, calls=%fused_computation.10 | convolution fusion | flops 2822242304 | bytes 9961472 | tf_op jit(solution)/shard_map/dot_general | solution.py:50
  356.6 5.9 %copy.20 = bf16[512,3584]{1,0:T(8,128)(2,1)} copy(bf16[512,3584]{0,1:T(8,128)(2,1)} %fusion.4) | data formatting | bytes 7340032
  362.5 25.8 %all-gather.8.cloned.1.call-done = bf16[768,3584]{1,0:T(8,128)(2,1)} async-done(((bf16[48,3584]{1,0:T(8,128)(2,1)}), bf16[768,3584]{1,0:T(8,128)(2,1)}) %all-gather.8.cloned.1.call-update) | async-done | bytes 5505040 | tf_op jit(solution)/shard_map/all_gather | solution.py:42
  388.3 7.1 %multiply_convert_fusion = bf16[3584,512]{1,0:T(8,128)(2,1)} fusion(bf16[768,3584]{1,0:T(8,128)(2,1)} %all-gather.8.cloned.1.call-done, bf16[768,512]{1,0:T(8,128)(2,1)S(1)} %all_gather.16), kind=kOutput, calls=%fused_computation.6 | convolution fusion | flops 2822242304 | bytes 9961472 | tf_op jit(solution)/shard_map/dot_general | solution.py:47
  395.4 27.2 %reduce-scatter.5.cloned.1.call-done = bf16[96,512]{1,0:T(8,128)(2,1)} async-done(((bf16[768,512]{1,0:T(8,128)(2,1)}), bf16[96,512]{1,0:T(8,128)(2,1)}) %reduce-scatter.5.cloned.1.call-update) | async-done | bytes 98320 | tf_op jit(solution)/shard_map/reduce_scatter | solution.py:66
Async XLA Ops:
  7.2 201.5 %reduce-scatter.7.cloned.1.call-start = ((), (), s32[]{:S(2)}) async-start(), calls=%async_computation.6 | async-start | bytes 17547264 | tf_op jit(solution)/shard_map/reduce_scatter | solution.py:35
  97.8 170.8 %all-gather.4.cloned.1.call-start = ((), (), s32[]{:S(2)}) async-start(), calls=%async_computation.2 | async-start | bytes 5849088 | tf_op jit(solution)/shard_map/all_gather | solution.py:43
  211.3 117.5 %all-gather.6.cloned.1.call-start = ((), (), s32[]{:S(2)}) async-start(), calls=%async_computation.3 | async-start | bytes 5849088 | tf_op jit(solution)/shard_map/all_gather | solution.py:44
  212.0 176.3 %all-gather.8.cloned.1.call-start = ((), (), s32[]{:S(2)}) async-start(), calls=%async_computation.5 | async-start | bytes 5849088 | tf_op jit(solution)/shard_map/all_gather | solution.py:42
  212.6 210.0 %reduce-scatter.5.cloned.1.call-start = ((), (), s32[]{:S(2)}) async-start(), calls=%async_computation.4 | async-start | bytes 884736 | tf_op jit(solution)/shard_map/reduce_scatter | solution.py:66
Sparse Core Ops, SparseCore 0:
  98.0 110.6 reduce-scatter.6
  211.6 57.0 all-gather.3
  271.6 57.2 all-gather.5
  331.1 57.2 all-gather.7
  391.3 31.3 reduce-scatter.4
where the time goes:
time: 430 us; the launch traced here: 429 us
  waiting for transfers between devices  275 us (64%)
  matrix products  56.3 us (13%)
  local copies, waits for them, and re-layouts  34.2 us (8%)
  blocking collectives  28.5 us (7%)
  other arithmetic  21.2 us (5%)
  between operations  13.8 us (3%)
    reduce_scatter x1, waiting for transfers between devices, local(): lax.psum_scatter(jnp.concatenate([gate_up, hidden_grad], axis=1).astype(j...  111 us
    all_gather x1, waiting for transfers between devices, local(): lax.all_gather(gate_delta, 'row', axis=0, tiled=True)  55.8 us
    all_gather x1, waiting for transfers between devices, local(): accumulate_up_delta = lax.all_gather(up_delta, 'row', axis=0, tiled=True)  54.1 us
    unnamed x3, local copies, waits for them, and re-layouts  34.2 us
    reduce_scatter x1, waiting for transfers between devices, local(): lax.psum_scatter(term.astype(jnp.bfloat16), 'col', scatter_dimension=0, t...  27.2 us
    all_gather x1, waiting for transfers between devices, local(): accumulate_hidden = lax.all_gather(hidden, 'row', axis=0, tiled=True)  25.8 us
    concatenate x1, other arithmetic, local(): jnp.concatenate([gate_up, hidden_grad], axis=1).astype(jnp.bfloat16)  18.5 us
    all_gather x1, blocking collectives, local(): lax.all_gather(layer_input, 'col', axis=0, tiled=True)  14.9 us
  transfers between devices with their start and end apart: 5, of which 5 were waited for; matrix products, arithmetic and copies ran while one was open for 11% of the time, Pallas kernels for 0%

commit v1 on v0

--- a/solution.py
+++ b/solution.py
@@ -39,8 +39,11 @@
         tiled=True,
     ).astype(jnp.float32)
     hidden, gate_delta, up_delta = swiglu_back(summed, width)
-    accumulate_hidden = lax.all_gather(hidden, "row", axis=0, tiled=True)
-    accumulate_gate_delta = lax.all_gather(gate_delta, "row", axis=0, tiled=True)
+    accumulate_hidden, accumulate_gate_delta = jnp.split(
+        lax.all_gather(jnp.concatenate([hidden, gate_delta], axis=1), "row", axis=0, tiled=True),
+        [hidden.shape[1]],
+        axis=1,
+    )
     accumulate_up_delta = lax.all_gather(up_delta, "row", axis=0, tiled=True)
     left = input_rows
     right = cot_rows

time: 430 us -> 401 us (0.933)
  waiting for transfers between devices: 275 us -> 243 us
    all_gather x2 -> x1, waiting for transfers between devices: 81.6 us -> 64.2 us  [local(): lax.all_gather(jnp.concatenate([hidden, gate_delta], axis=1), 'row', axis...]
    reduce_scatter x1, waiting for transfers between devices: 27.2 us -> 11.2 us  [local(): lax.psum_scatter(term.astype(jnp.bfloat16), 'col', scatter_dimension=0, t...]
  transfers between devices with their start and end apart: 5 -> 4, of which waited for: 5 -> 4; matrix products, arithmetic and copies ran while one was open for 11% -> 11% of each run, Pallas kernels for 0% -> 0%
where the time goes in v1:
time: 401 us; the launch traced here: 400 us
  waiting for transfers between devices  243 us (61%)
  matrix products  58.7 us (15%)
  local copies, waits for them, and re-layouts  34.1 us (9%)
  blocking collectives  28.5 us (7%)
  other arithmetic  21.8 us (5%)
  between operations  13.8 us (3%)
    reduce_scatter x1, waiting for transfers between devices, local(): lax.psum_scatter(jnp.concatenate([gate_up, hidden_grad], axis=1).astype(j...  111 us
    all_gather x1, waiting for transfers between devices, local(): lax.all_gather(jnp.concatenate([hidden, gate_delta], axis=1), 'row', axis...  64.2 us
    all_gather x1, waiting for transfers between devices, local(): accumulate_up_delta = lax.all_gather(up_delta, 'row', axis=0, tiled=True)  56.4 us
    unnamed x3, local copies, waits for them, and re-layouts  34.1 us
    concatenate x1, other arithmetic, local(): jnp.concatenate([gate_up, hidden_grad], axis=1).astype(jnp.bfloat16)  18.5 us
    all_gather x1, blocking collectives, local(): lax.all_gather(layer_input, 'col', axis=0, tiled=True)  14.9 us
    dot_general x1, matrix products, local(): gate_up = jnp.dot(left, both_weights, preferred_element_type=jnp.float32)  13.8 us
    all_gather x1, blocking collectives, local(): lax.all_gather(out_grad, 'col', axis=0, tiled=True)  13.6 us
  transfers between devices with their start and end apart: 4, of which 4 were waited for; matrix products, arithmetic and copies ran while one was open for 11% of the time, Pallas kernels for 0%

profile of v1, /device:TPU:0, one launch (start us, length us, event | category | flops | bytes accessed | tf_op | source)
XLA Modules:
  0.0 399.9 jit_solution(1978704232832963677)
XLA Ops:
  7.2 0.0 reduce-scatter.7.cloned.1.call-start
  7.2 14.9 %all_gather.12 = bf16[768,512]{1,0:T(8,128)(2,1)S(1)} all-gather(bf16[96,512]{1,0:T(8,128)(2,1)} %param.5), channel_id=1, replica_groups=mesh['row'=16,'col'=8] {'col'}, dimensions={0}, use_global_device_ids=true | all-gather | bytes 884736 | tf_op jit(solution)/shard_map/all_gather | solution.py:21
  22.1 13.6 %all_gather.13 = bf16[768,512]{1,0:T(8,128)(2,1)S(1)} all-gather(bf16[96,512]{1,0:T(8,128)(2,1)} %param.6), channel_id=1, replica_groups=mesh['row'=16,'col'=8] {'col'}, dimensions={0}, use_global_device_ids=true | all-gather | bytes 884736 | tf_op jit(solution)/shard_map/all_gather | solution.py:22
  35.7 7.5 %convolution_convert_fusion.1 = bf16[768,3584]{0,1:T(8,128)(2,1)} fusion(bf16[768,512]{1,0:T(8,128)(2,1)S(1)} %all_gather.13, bf16[3584,512]{1,0:T(8,128)(2,1)} %param.9), kind=kOutput, calls=%fused_computation.9 | convolution fusion | flops 2821324800 | bytes 9961472 | tf_op jit(solution)/shard_map/dot_general | solution.py:32
  43.2 13.8 %fusion = bf16[768,7168]{0,1:T(8,128)(2,1)} fusion(bf16[768,512]{1,0:T(8,128)(2,1)S(1)} %all_gather.12, bf16[512,3584]{1,0:T(8,128)(2,1)} %param.8, bf16[512,3584]{1,0:T(8,128)(2,1)} %param.7), kind=kOutput, calls=%fused_computation.2 | convolution fusion | flops 5657329664 | bytes 19136512 | tf_op jit(solution)/shard_map/dot_general | solution.py:31
  57.0 18.5 %pad_maximum_fusion = bf16[768,10752]{0,1:T(8,128)(2,1)} fusion(bf16[768,3584]{0,1:T(8,128)(2,1)} %convolution_convert_fusion.1, bf16[768,7168]{0,1:T(8,128)(2,1)} %fusion), kind=kLoop, calls=%fused_computation | loop fusion | flops 33030144 | bytes 33030144 | tf_op jit(solution)/shard_map/concatenate | solution.py:36
  75.5 22.3 %copy.23 = bf16[768,10752]{1,0:T(8,128)(2,1)} copy(bf16[768,10752]{0,1:T(8,128)(2,1)} %pad_maximum_fusion) | data formatting | bytes 33030144
  97.8 0.0 reduce-scatter.7.cloned.1.call-update
  97.8 0.0 all-gather.5.cloned.1.call-start
  97.8 110.7 %reduce-scatter.7.cloned.1.call-done = bf16[48,10752]{1,0:T(8,128)(2,1)} async-done(((bf16[768,10752]{1,0:T(8,128)(2,1)}), bf16[48,10752]{1,0:T(8,128)(2,1)}) %reduce-scatter.7.cloned.1.call-update) | async-done | bytes 1032208 | tf_op jit(solution)/shard_map/reduce_scatter | solution.py:35
  208.5 1.4 convert_element_type.31
  209.9 1.1 multiply_convert_fusion.5
  211.0 0.0 all-gather.5.cloned.1.call-update
  211.0 0.0 all-gather.3.cloned.1.call-start
  211.0 0.9 pad_maximum_fusion.1
  211.9 0.0 all-gather.3.cloned.1.call-update
  212.0 0.2 reduce-scatter.5.cloned.1.call-start
  212.2 56.4 %all-gather.5.cloned.1.call-done = bf16[768,3584]{1,0:T(8,128)(2,1)} async-done(((bf16[48,3584]{1,0:T(8,128)(2,1)}), bf16[768,3584]{1,0:T(8,128)(2,1)}) %all-gather.5.cloned.1.call-update) | async-done | bytes 5505040 | tf_op jit(solution)/shard_map/all_gather | solution.py:47
  268.6 7.1 %fusion.6 = bf16[512,3584]{0,1:T(8,128)(2,1)} fusion(bf16[768,3584]{1,0:T(8,128)(2,1)} %all-gather.5.cloned.1.call-done, bf16[768,512]{1,0:T(8,128)(2,1)S(1)} %all_gather.12), kind=kOutput, calls=%fused_computation.12 | convolution fusion | flops 2822242304 | bytes 9961472 | tf_op jit(solution)/shard_map/dot_general | solution.py:56
  275.7 5.9 %copy.21 = bf16[512,3584]{1,0:T(8,128)(2,1)} copy(bf16[512,3584]{0,1:T(8,128)(2,1)} %fusion.6) | data formatting | bytes 7340032
  281.6 8.1 %fusion.14 = f32[768,512]{1,0:T(8,128)} fusion(bf16[768,3584]{1,0:T(8,128)(2,1)} %all-gather.5.cloned.1.call-done, bf16[512,3584]{1,0:T(8,128)(2,1)} %param.8), kind=kOutput, calls=%fused_computation.24 | convolution fusion | flops 2818572288 | bytes 10747904 | tf_op jit(solution)/shard_map/dot_general | solution.py:62
  289.6 64.2 %all-gather.3.cloned.1.call-done = bf16[768,7168]{1,0:T(8,128)(2,1)} async-done(((bf16[48,7168]{1,0:T(8,128)(2,1)}), bf16[768,7168]{1,0:T(8,128)(2,1)}) %all-gather.3.cloned.1.call-update) | async-done | bytes 11010064 | tf_op jit(solution)/shard_map/all_gather | solution.py:43
  353.9 8.0 %add_convert_fusion = bf16[768,512]{1,0:T(8,128)(2,1)} fusion(f32[768,512]{1,0:T(8,128)} %fusion.14, bf16[512,3584]{1,0:T(8,128)(2,1)} %param.7, bf16[768,7168]{1,0:T(8,128)(2,1)} %all-gather.3.cloned.1.call-done), kind=kOutput, calls=%fused_computation.16 | convolution fusion | flops 2819358720 | bytes 11534336 | tf_op jit(solution)/shard_map/dot_general | solution.py:59
  361.9 0.0 reduce-scatter.5.cloned.1.call-update
  361.9 7.1 %fusion.5 = bf16[512,3584]{0,1:T(8,128)(2,1)} fusion(bf16[768,512]{1,0:T(8,128)(2,1)S(1)} %all_gather.12, bf16[768,7168]{1,0:T(8,128)(2,1)} %all-gather.3.cloned.1.call-done), kind=kOutput, calls=%fused_computation.11 | convolution fusion | flops 2822242304 | bytes 9961472 | tf_op jit(solution)/shard_map/dot_general | solution.py:53
  369.0 5.9 %copy.20 = bf16[512,3584]{1,0:T(8,128)(2,1)} copy(bf16[512,3584]{0,1:T(8,128)(2,1)} %fusion.5) | data formatting | bytes 7340032
  375.0 7.1 %multiply_convert_fusion = bf16[3584,512]{1,0:T(8,128)(2,1)} fusion(bf16[768,512]{1,0:T(8,128)(2,1)S(1)} %all_gather.13, bf16[768,7168]{1,0:T(8,128)(2,1)} %all-gather.3.cloned.1.call-done), kind=kOutput, calls=%fused_computation.6 | convolution fusion | flops 2822242304 | bytes 9961472 | tf_op jit(solution)/shard_map/dot_general | solution.py:50
  382.1 11.2 %reduce-scatter.5.cloned.1.call-done = bf16[96,512]{1,0:T(8,128)(2,1)} async-done(((bf16[768,512]{1,0:T(8,128)(2,1)}), bf16[96,512]{1,0:T(8,128)(2,1)}) %reduce-scatter.5.cloned.1.call-update) | async-done | bytes 98320 | tf_op jit(solution)/shard_map/reduce_scatter | solution.py:69
Async XLA Ops:
  7.2 201.4 %reduce-scatter.7.cloned.1.call-start = ((), (), s32[]{:S(2)}) async-start(), calls=%async_computation.5 | async-start | bytes 17547264 | tf_op jit(solution)/shard_map/reduce_scatter | solution.py:35
  97.8 170.8 %all-gather.5.cloned.1.call-start = ((), (), s32[]{:S(2)}) async-start(), calls=%async_computation.3 | async-start | bytes 5849088 | tf_op jit(solution)/shard_map/all_gather | solution.py:47
  211.0 142.9 %all-gather.3.cloned.1.call-start = ((), (), s32[]{:S(2)}) async-start(), calls=%async_computation.2 | async-start | bytes 11698176 | tf_op jit(solution)/shard_map/all_gather | solution.py:43
  212.0 181.4 %reduce-scatter.5.cloned.1.call-start = ((), (), s32[]{:S(2)}) async-start(), calls=%async_computation.4 | async-start | bytes 884736 | tf_op jit(solution)/shard_map/reduce_scatter | solution.py:69
Sparse Core Ops, SparseCore 0:
  97.9 110.5 reduce-scatter.6
  211.5 57.0 all-gather.4
  271.5 82.3 all-gather.2
  362.0 31.2 reduce-scatter.4
